TPU v7x, 256 devices: a whole 4x4x8 slice. The times are simulated.
256 devices in a mesh: rows: 64 (over x, z, core), cols: 4 (over y).
Axes of the slice: x: 4, y: 4, z: 8, core: 2. Of those that a mesh axis runs over, the one named last changes fastest.
Arguments:
- operator_blocks: bfloat16 [8, 64, 64, 16384], P(None, None, None, 'rows'), may hold values from -0.75 to 0.75
- tentative: bfloat16 [64, 64, 16384], P(None, 'cols', 'rows'), may hold values from -1.5 to 1.5
- jacobi_scale: bfloat16 [64, 16384], P(None, 'rows'), may hold values from 0.29882812 to 1.1953125
- columns: int32 [8, 16384], P(None, 'rows'), may hold values from 0 to 16383, as said below
Outputs:
- prolongator: bfloat16 [64, 64, 16384], P(None, 'cols', 'rows')
- coarse_diag: float32 [64, 64, 16384], P('cols', None, 'rows')
- coarse_off: bfloat16 [64, 6, 64, 16384], P('cols', None, None, 'rows')
Inputs may be any that keep to these rules, and one draw needn't show every extreme that they name: Rows number the elements of a periodic grid of 8 x 16 x (2 * 64) elements, first dimension fastest; each device holds 2 whole layers. columns[0, i] is i. columns[1, i] is the partner of i in a perfect matching (its partner is i again): either the neighbour of i along the first dimension on the same device, or a row on the device 64 / 2 indices away along rows, or a row on the device whose index along rows differs in the lowest bit. columns[2 .. 7, i] are the six face neighbours of i, in the order minus first, plus first, minus second, plus second, minus third, plus third dimension. `columns`: for two different devices along rows, the pairs with one row on each number either zero or exactly 2; every draw has such a pair of devices with 2.
All inputs are finite; a program needn't handle non-finite values.
Results may differ from a plain program's by a relative error of at most 0.0064.
Values may be sent and summed in bfloat16 or wider, within the bound.
A program may use at most 192 MiB of HBM per device.

v0:
```python
import jax
import jax.numpy as jnp
from jax import lax
from jax.sharding import PartitionSpec as P

CAP = 2
HALO = 128


def laid_out(parts, dim):
    parts = jnp.moveaxis(parts, 0, dim)
    lengths = parts.shape
    return parts.reshape(*lengths[:dim], lengths[dim] * lengths[dim + 1], *lengths[dim + 2 :])


def from_everyone(value, axis):
    copies = jnp.broadcast_to(value, (lax.axis_size(axis), *value.shape))
    return lax.all_to_all(copies, axis, split_axis=0, concat_axis=0, tiled=True)


def gathered_copies(value, axis, dim):
    return laid_out(from_everyone(value, axis), dim)


def with_halo(block, sides, width):
    for axis, dim in sides:
        count = lax.axis_size(axis)
        forward = [(i, i + 1) for i in range(count - 1)]
        forward.append((count - 1, 0))
        backward = [(target, source) for source, target in forward]
        low = lax.ppermute(
            lax.slice_in_dim(block, block.shape[dim] - width, None, axis=dim), axis, forward
        )
        high = lax.ppermute(lax.slice_in_dim(block, 0, width, axis=dim), axis, backward)
        block = jnp.concatenate([low, block, high], axis=dim)
    return block


def build_plan(columns, devices, device_id):
    row_count = columns.shape[1]
    row_ids = jnp.arange(row_count, dtype=jnp.int32)
    partner = columns[1]
    owners = partner // row_count
    remote = owners != device_id
    same_owner = (owners[:, None] == owners[None, :]) & remote[:, None] & remote[None, :]
    send_order = jnp.sum(same_owner & (row_ids[None, :] < row_ids[:, None]), axis=1)
    recv_order = jnp.sum(same_owner & (partner[None, :] < partner[:, None]), axis=1)
    target = jnp.where(remote, owners * CAP + send_order, devices * CAP)
    send_slots = jnp.zeros((devices * CAP,), jnp.int32).at[target].set(row_ids, mode="drop")
    read_slots = jnp.where(
        remote, row_count + owners * CAP + recv_order, partner - device_id * row_count
    )
    return (send_slots, read_slots)


def pack_rows(blocks, send_slots, devices):
    matrix = blocks.reshape(-1, blocks.shape[-1])
    return jnp.take(matrix, send_slots, axis=1).reshape(matrix.shape[0], devices, -1)


def unpack_rows(blocks, received, read_slots):
    matrix = blocks.reshape(-1, blocks.shape[-1])
    joined = jnp.concatenate([matrix, received.reshape(matrix.shape[0], -1)], axis=1)
    return jnp.take(joined, read_slots, axis=1).reshape(blocks.shape)


def smooth(pair_blocks, scale_rows, tent_self, tent_other):
    coupled = jnp.einsum(
        "fgx,gcx->fcx", pair_blocks[0], tent_self, preferred_element_type=jnp.float32
    )
    coupled = coupled + jnp.einsum(
        "fgx,gcx->fcx", pair_blocks[1], tent_other, preferred_element_type=jnp.float32
    )
    return (
        tent_self.astype(jnp.float32) - scale_rows.astype(jnp.float32)[:, None, :] * coupled
    ).astype(jnp.bfloat16)


def coarse_terms(left_full, coupling, right_part):
    reached = jnp.einsum(
        "kfgx,gckx->kfcx", coupling, right_part, preferred_element_type=jnp.float32
    ).astype(jnp.bfloat16)
    return jnp.einsum("fax,kfcx->ckax", left_full, reached, preferred_element_type=jnp.float32)


def on_device(operator_blocks, tentative, jacobi_scale, columns):
    row_count = columns.shape[1]
    devices = lax.axis_size("rows")
    device_id = lax.axis_index("rows")
    send_slots, read_slots = build_plan(columns, devices, device_id)
    pair_self = operator_blocks[:2]
    tent_in = lax.all_to_all(
        pack_rows(tentative, send_slots, devices), "rows", split_axis=1, concat_axis=1, tiled=True
    )
    tent_other = unpack_rows(tentative, tent_in, read_slots)
    prolongator = smooth(pair_self, jacobi_scale, tentative, tent_other)
    prolong_in = lax.all_to_all(
        pack_rows(prolongator, send_slots, devices), "rows", split_axis=1, concat_axis=1, tiled=True
    )
    prolong_other = unpack_rows(prolongator, prolong_in, read_slots)
    full_self = gathered_copies(prolongator, "cols", 1)
    rim_width = min(HALO, row_count)
    extended = with_halo(prolongator, (("rows", 2),), rim_width)
    source = jnp.concatenate([extended, prolong_other], axis=2)
    local_rows = jnp.arange(row_count, dtype=jnp.int32)
    total_rows = row_count * devices
    neighbour_pos = jnp.mod(columns[2:] - device_id * row_count + rim_width, total_rows)
    positions = jnp.concatenate(
        [
            (rim_width + local_rows)[None, :],
            (extended.shape[2] + local_rows)[None, :],
            neighbour_pos,
        ],
        axis=0,
    )
    picked = jnp.take(source, positions.reshape(-1), axis=2).reshape(
        source.shape[0], source.shape[1], -1, row_count
    )
    contributions = coarse_terms(full_self, operator_blocks, picked)
    coarse_off = contributions[:, 2:].astype(jnp.bfloat16)
    own_sum = contributions[:, 0] + contributions[:, 1]
    sum_in = lax.all_to_all(
        pack_rows(own_sum, send_slots, devices).astype(jnp.bfloat16),
        "rows",
        split_axis=1,
        concat_axis=1,
        tiled=True,
    ).astype(jnp.float32)
    other_sum = unpack_rows(own_sum, sum_in, read_slots)
    return (prolongator, own_sum + other_sum, coarse_off)


def solution(mesh):
    placed = (
        P(None, None, None, "rows"),
        P(None, "cols", "rows"),
        P(None, "rows"),
        P(None, "rows"),
    )
    return jax.shard_map(
        on_device,
        mesh=mesh,
        in_specs=placed,
        out_specs=(P(None, "cols", "rows"), P("cols", None, "rows"), P("cols", None, None, "rows")),
        check_vma=False,
    )
```

profile of v0, /device:TPU:4, one launch (start us, length us, event | category | flops | bytes accessed | tf_op | source)
XLA Modules:
  0.0 240.1 jit_solution(7600153242309810046)
XLA Ops:
  7.6 12.1 %all-to-all-start = ((bf16[1024,64,2]{0,2,1:T(2,128)(2,1)}), bf16[1024,64,2]{0,2,1:T(2,128)(2,1)S(1)}, u32[]{:S(2)}, u32[]{:S(2)}) async-start(bf16[1024,64,2]{0,2,1:T(2,128)(2,1)} %reshape.296), calls=%async_computation | async-start | bytes 524288 | tf_op jit(solution)/shard_map/all_to_all | solution.py:92
  19.7 4.1 %fusion.22 = (bf16[1,64,64,256]{3,2,1,0:T(8,128)(2,1)S(1)}, bf16[1,64,64,256]{3,2,1,0:T(8,128)(2,1)}) fusion(bf16[8,64,64,256]{3,2,1,0:T(8,128)(2,1)} %param.8), kind=kLoop, calls=%fused_computation.81 | loop fusion | bytes 8388608 | tf_op jit(solution)/shard_map/slice | solution.py:69
  25.9 46.0 %copy.86 = bf16[8,64,64,256]{2,1,0,3:T(8,128)(2,1)} copy(bf16[8,64,64,256]{3,2,1,0:T(8,128)(2,1)} %param.8) | data formatting | bytes 33554432 | tf_op args[0]
  72.0 7.6 %copy.102 = bf16[1,64,64,256]{2,1,3,0:T(8,128)(2,1)} copy(bf16[1,64,64,256]{3,2,1,0:T(8,128)(2,1)} %get-tuple-element.28) | data formatting | bytes 4194304
  79.6 6.7 %copy.101 = bf16[1,64,64,256]{2,1,3,0:T(8,128)(2,1)} copy(bf16[1,64,64,256]{3,2,1,0:T(8,128)(2,1)S(1)} %get-tuple-element.27) | data formatting | bytes 4194304
  89.4 4.6 %fusion.5 = f32[256,16,64]{2,1,0:T(8,128)S(1)} fusion(bf16[64,16,256]{0,1,2:T(8,128)(2,1)S(1)} %copy.78, bf16[1,64,64,256]{2,1,3,0:T(8,128)(2,1)} %copy.102), kind=kOutput, calls=%fused_computation.15 | convolution fusion | flops 33554432 | bytes 3670016 | tf_op jit(solution)/shard_map/fgx,gcx->fcx/dot_general | solution.py:71
  94.0 2.3 fusion.12
  99.7 10.3 %all-to-all-start.1 = ((bf16[1024,64,2]{0,2,1:T(2,128)(2,1)}), bf16[1024,64,2]{0,2,1:T(2,128)(2,1)S(1)}, u32[]{:S(2)}, u32[]{:S(2)}) async-start(bf16[1024,64,2]{0,2,1:T(2,128)(2,1)} %reshape.300), calls=%async_computation.1 | async-start | bytes 524288 | tf_op jit(solution)/shard_map/all_to_all | solution.py:97
  110.2 11.3 %all-to-all-done.1 = bf16[1024,64,2]{0,2,1:T(2,128)(2,1)S(1)} async-done(((bf16[1024,64,2]{0,2,1:T(2,128)(2,1)}), bf16[1024,64,2]{0,2,1:T(2,128)(2,1)S(1)}, u32[]{:S(2)}, u32[]{:S(2)}) %all-to-all-start.1) | async-done | bytes 262176 | tf_op jit(solution)/shard_map/all_to_all | solution.py:97
  123.0 4.5 %all-to-all-start.2 = ((bf16[4,64,16,256]{3,2,1,0:T(8,128)(2,1)}), bf16[4,64,16,256]{3,2,1,0:T(8,128)(2,1)}, u32[]{:S(2)}, u32[]{:S(2)}) async-start(bf16[4,64,16,256]{3,2,1,0:T(8,128)(2,1)} %broadcast_in_dim.79), calls=%async_computation.2 | async-start | bytes 4194304 | tf_op jit(solution)/shard_map/all_to_all | solution.py:18
  127.9 3.7 %collective-permute-start.1 = (bf16[64,16,128]{0,1,2:T(8,128)(2,1)S(1)}, bf16[64,16,128]{0,1,2:T(8,128)(2,1)}, u32[]{:S(2)}, u32[]{:S(2)}) collective-permute-start(bf16[64,16,128]{0,1,2:T(8,128)(2,1)S(1)} %get-tuple-element.30), channel_id=1, source_target_pairs={{4,0},{8,4},{12,8},{16,12},{20,16},{24,20},{28,24},{32,28},{36,32}... | collective-permute-start | bytes 786440 | tf_op jit(solution)/shard_map/ppermute | solution.py:34
  133.3 2.2 copy.84
  135.5 3.0 %collective-permute-done = bf16[64,16,128]{0,1,2:T(8,128)(2,1)S(1)} collective-permute-done((bf16[64,16,128]{0,1,2:T(8,128)(2,1)S(1)}, bf16[64,16,128]{0,1,2:T(8,128)(2,1)S(1)}, u32[]{:S(2)}, u32[]{:S(2)}) %collective-permute-start) | collective-permute-done | bytes 262176 | tf_op jit(solution)/shard_map/ppermute | solution.py:31
  139.3 2.3 pad_maximum_fusion
  141.6 16.2 %gather_fusion = bf16[2048,64,16]{1,2,0:T(8,128)(2,1)} fusion(bf16[64,16,768]{0,1,2:T(8,128)(2,1)S(1)} %pad_maximum_fusion, s32[2048]{0:T(1024)S(1)} %broadcast_clamp_fusion), kind=kCustom, calls=%fused_computation.4 | custom fusion | bytes 8396800 | tf_op jit(solution)/shard_map/jit(_take)/gather | solution.py:116
  159.7 6.7 %copy.98 = bf16[64,64,256,1]{1,0,3,2:T(8,128)(2,1)} copy(bf16[64,64,256,1]{2,1,0,3:T(8,128)(2,1)S(1)} %bitcast.86) | data formatting | bytes 4194304 | tf_op jit(solution)/shard_map/reshape | solution.py:13
  166.4 28.1 %convolution_bitcast_fusion = f32[16,8,64,256]{2,0,1,3:T(8,128)} fusion(bf16[64,64,256,1]{1,0,3,2:T(8,128)(2,1)} %copy.98, bf16[8,64,64,256]{2,1,0,3:T(8,128)(2,1)} %copy.86, bf16[64,16,8,256]{0,1,3,2:T(8,128)(2,1)} %bitcast.85, pred[8,256]{0,1:T(8,128)(4,1)S(1)} %copy.79), kind=kOutput, calls=%fused_computation.9 | convolution fusion | flops 541065216 | bytes 31459328 | tf_op jit(solution)/shard_map/fax,kfcx->ckax/dot_general | solution.py:83
  194.5 2.5 %slice_add_fusion = f32[16,1,64,256]{2,0,1,3:T(8,128)S(1)} fusion(f32[16,8,64,256]{2,0,1,3:T(8,128)} %convolution_bitcast_fusion), kind=kLoop, calls=%fused_computation.21 | loop fusion | flops 262144 | bytes 3145728 | tf_op jit(solution)/shard_map/add | solution.py:121
  202.5 8.3 %all-to-all-start.3 = ((bf16[1024,64,2]{0,2,1:T(2,128)(2,1)}), bf16[1024,64,2]{0,2,1:T(2,128)(2,1)S(1)}, u32[]{:S(2)}, u32[]{:S(2)}) async-start(bf16[1024,64,2]{0,2,1:T(2,128)(2,1)} %select_convert_fusion), calls=%async_computation.3 | async-start | bytes 524288 | tf_op jit(solution)/shard_map/all_to_all | solution.py:122
  210.8 8.7 %slice.68 = bf16[16,6,64,256]{2,0,1,3:T(8,128)(2,1)} slice(f32[16,8,64,256]{2,0,1,3:T(8,128)} %convolution_bitcast_fusion), slice={[0:16], [2:8], [0:64], [0:256]} | slice | bytes 6291456 | tf_op jit(solution)/shard_map/slice | solution.py:120
  219.5 8.2 %copy.97 = bf16[16,6,64,256]{3,2,1,0:T(8,128)(2,1)} copy(bf16[16,6,64,256]{2,0,1,3:T(8,128)(2,1)} %slice.68) | data formatting | bytes 6291456
  230.4 2.5 %copy.94 = f32[16,64,256]{1,0,2:T(8,128)S(1)} copy(f32[16,64,256]{2,1,0:T(8,128)} %bitcast.90) | data formatting | bytes 2097152 | tf_op jit(solution)/shard_map/jit(_take)/gather | solution.py:64
  233.0 3.7 %bitcast_add_fusion = f32[16,64,256]{1,0,2:T(8,128)} fusion(f32[16,64,256]{1,0,2:T(8,128)S(1)} %copy.94, pred[256]{0:T(512)(128)(4,1)S(1)} %get-tuple-element.21, f32[16,8,64,256]{2,0,1,3:T(8,128)} %convolution_bitcast_fusion), kind=kLoop, calls=%fused_computation.22 | loop fusion | flops 786432 | bytes 4194560 | tf_op jit(solution)/shard_map/add | solution.py:130
  236.6 3.5 %copy.96 = f32[16,64,256]{2,1,0:T(8,128)} copy(f32[16,64,256]{1,0,2:T(8,128)} %bitcast_add_fusion) | data formatting | bytes 2097152
  (78 shorter events, 30.1 us)
Async XLA Ops:
  7.6 78.8 %all-to-all-start = ((bf16[1024,64,2]{0,2,1:T(2,128)(2,1)}), bf16[1024,64,2]{0,2,1:T(2,128)(2,1)S(1)}, u32[]{:S(2)}, u32[]{:S(2)}) async-start(bf16[1024,64,2]{0,2,1:T(2,128)(2,1)} %reshape.296), calls=%async_computation | async-start | bytes 524288 | tf_op jit(solution)/shard_map/all_to_all | solution.py:92
  19.7 4.1 %copy-start.4 = (bf16[64,16,256]{2,1,0:T(8,128)(2,1)S(1)}, bf16[64,16,256]{2,1,0:T(8,128)(2,1)}, u32[]{:S(2)}) copy-start(bf16[64,16,256]{2,1,0:T(8,128)(2,1)} %param.9) | copy-start | bytes 1572868
  79.6 6.7 %copy-start.6 = (bf16[64,256]{1,0:T(8,128)(2,1)S(1)}, bf16[64,256]{1,0:T(8,128)(2,1)}, u32[]{:S(2)}) copy-start(bf16[64,256]{1,0:T(8,128)(2,1)} %param.10) | copy-start | bytes 98308
  89.4 4.6 %copy-start = (bf16[1,64,64,256]{2,1,3,0:T(8,128)(2,1)S(1)}, bf16[1,64,64,256]{2,1,3,0:T(8,128)(2,1)}, u32[]{:S(2)}) copy-start(bf16[1,64,64,256]{2,1,3,0:T(8,128)(2,1)} %copy.101) | copy-start | bytes 6291460
  89.4 4.6 %copy-start.3 = (bf16[64,16,256]{0,1,2:T(8,128)(2,1)S(1)}, bf16[64,16,256]{0,1,2:T(8,128)(2,1)}, u32[]{:S(2)}) copy-start(bf16[64,16,256]{0,1,2:T(8,128)(2,1)} %copy.70) | copy-start | bytes 1572868
  96.3 31.2 %copy-start.1 = (bf16[64,16,256]{0,1,2:T(8,128)(2,1)}, bf16[64,16,256]{0,1,2:T(8,128)(2,1)S(1)}, u32[]{:S(2)}) copy-start(bf16[64,16,256]{0,1,2:T(8,128)(2,1)S(1)} %fusion.12) | copy-start | bytes 1572868
  96.3 13.7 %copy-start.7 = (s32[8,256]{1,0:T(8,128)S(1)}, s32[8,256]{1,0:T(8,128)}, u32[]{:S(2)}) copy-start(s32[8,256]{1,0:T(8,128)} %param.11) | copy-start | bytes 24580
  97.7 25.3 %copy-start.2 = (bf16[64,16,256]{2,1,0:T(8,128)(2,1)}, bf16[64,16,256]{2,1,0:T(8,128)(2,1)S(1)}, u32[]{:S(2)}) copy-start(bf16[64,16,256]{2,1,0:T(8,128)(2,1)S(1)} %copy.95) | copy-start | bytes 1572868
  99.7 21.9 %all-to-all-start.1 = ((bf16[1024,64,2]{0,2,1:T(2,128)(2,1)}), bf16[1024,64,2]{0,2,1:T(2,128)(2,1)S(1)}, u32[]{:S(2)}, u32[]{:S(2)}) async-start(bf16[1024,64,2]{0,2,1:T(2,128)(2,1)} %reshape.300), calls=%async_computation.1 | async-start | bytes 524288 | tf_op jit(solution)/shard_map/all_to_all | solution.py:97
  123.0 34.8 %all-to-all-start.2 = ((bf16[4,64,16,256]{3,2,1,0:T(8,128)(2,1)}), bf16[4,64,16,256]{3,2,1,0:T(8,128)(2,1)}, u32[]{:S(2)}, u32[]{:S(2)}) async-start(bf16[4,64,16,256]{3,2,1,0:T(8,128)(2,1)} %broadcast_in_dim.79), calls=%async_computation.2 | async-start | bytes 4194304 | tf_op jit(solution)/shard_map/all_to_all | solution.py:18
  127.7 10.8 %collective-permute-start = (bf16[64,16,128]{0,1,2:T(8,128)(2,1)S(1)}, bf16[64,16,128]{0,1,2:T(8,128)(2,1)S(1)}, u32[]{:S(2)}, u32[]{:S(2)}) collective-permute-start(bf16[64,16,128]{0,1,2:T(8,128)(2,1)S(1)} %get-tuple-element.29), channel_id=1, source_target_pairs={{0,4},{4,8},{8,12},{12,16},{16,20},{20,24},{24,28},{28,32},{32,36}... | collective-permute-start | bytes 786440 | tf_op jit(solution)/shard_map/ppermute | solution.py:31
  127.9 11.4 %collective-permute-start.1 = (bf16[64,16,128]{0,1,2:T(8,128)(2,1)S(1)}, bf16[64,16,128]{0,1,2:T(8,128)(2,1)}, u32[]{:S(2)}, u32[]{:S(2)}) collective-permute-start(bf16[64,16,128]{0,1,2:T(8,128)(2,1)S(1)} %get-tuple-element.30), channel_id=1, source_target_pairs={{4,0},{8,4},{12,8},{16,12},{20,16},{24,20},{28,24},{32,28},{36,32}... | collective-permute-start | bytes 786440 | tf_op jit(solution)/shard_map/ppermute | solution.py:34
  138.5 0.8 copy-start.5
  202.5 25.3 %all-to-all-start.3 = ((bf16[1024,64,2]{0,2,1:T(2,128)(2,1)}), bf16[1024,64,2]{0,2,1:T(2,128)(2,1)S(1)}, u32[]{:S(2)}, u32[]{:S(2)}) async-start(bf16[1024,64,2]{0,2,1:T(2,128)(2,1)} %select_convert_fusion), calls=%async_computation.3 | async-start | bytes 524288 | tf_op jit(solution)/shard_map/all_to_all | solution.py:122
where the time goes:
time: 243 us; the launch traced here: 240 us
  local copies, waits for them, and re-layouts  139 us (57%)
  starting transfers between devices  39.1 us (16%)
  matrix products  35 us (14%)
  waiting for transfers between devices  14.3 us (6%)
  other arithmetic  12.1 us (5%)
    unnamed x24, local copies, waits for them, and re-layouts  76.3 us
    dot_general x1, matrix products, coarse_terms(): jnp.einsum('fax,kfcx->ckax', left_full, reached, preferred_element_type=j...  28.1 us
    gather x1, local copies, waits for them, and re-layouts, on_device(): jnp.take(source, positions.reshape(-1), axis=2)  16.2 us
    all_to_all x1, starting transfers between devices, on_device(): lax.all_to_all(pack_rows(tentative, send_slots, devices), 'rows', split_a...  12.1 us
    all_to_all x1, waiting for transfers between devices, on_device(): lax.all_to_all(pack_rows(prolongator, send_slots, devices), 'rows', split...  11.3 us
    all_to_all x1, starting transfers between devices, on_device(): lax.all_to_all(pack_rows(prolongator, send_slots, devices), 'rows', split...  10.3 us
    slice x1, local copies, waits for them, and re-layouts, on_device(): coarse_off = contributions[:, 2:].astype(jnp.bfloat16)  8.71 us
    all_to_all x1, starting transfers between devices, on_device(): lax.all_to_all(pack_rows(own_sum, send_slots, devices).astype(jnp.bfloat1...  8.3 us
  transfers between devices with their start and end apart: 6, of which 2 were waited for; matrix products, arithmetic and copies ran while one was open for 44% of the time, Pallas kernels for 0%

commit v1 on v0

v1 whole, which is shorter than its diff:
```python
import functools

import jax
import jax.numpy as jnp
from jax import lax
from jax.experimental import pallas as pl
from jax.experimental.pallas import tpu as pltpu
from jax.sharding import PartitionSpec as P

GX = 8
GY = 16
LAYER = GX * GY
BS = 64
PART = 16
STRIDE = LAYER + 8
CSTRIDE = 392
BIG = 1 << 20
MESH = pl.DeviceIdType.MESH
F32 = jnp.float32
BF16 = jnp.bfloat16
NT = (((1,), (1,)), ((), ()))
TN = (((0,), (0,)), ((), ()))


def iota(shape, dim):
    return lax.broadcasted_iota(jnp.int32, shape, dim)


def group_rows(block):
    return pl.ds(pl.multiple_of(block * STRIDE, 8), LAYER)


def of_position(position):
    return pl.ds(position, BS, stride=STRIDE)


def loop(count, unroll, body):
    def step(index, carry):
        for inner in range(unroll):
            body(index * unroll + inner)
        return carry

    lax.fori_loop(0, count // unroll, step, 0)


def relay(stage, target):
    def body(fine):
        for half in range(2):
            block = stage[:, fine, :, half * LAYER : (half + 1) * LAYER].reshape(128, LAYER)
            target[half, group_rows(fine), :] = block.T.astype(F32)

    loop(BS, 8, body)


def spread(rows_of, target):
    def body(fine):
        target[group_rows(fine), :] = jnp.concatenate(rows_of(fine), axis=0).T.astype(F32)

    loop(BS, 8, body)


def halves(ref, index):
    return ref[index, :, :LAYER], ref[index, :, LAYER:]


def left_of(ax, pair, position):
    return jnp.concatenate(
        [ax[pair, half, of_position(position), :] for half in range(2)], axis=0
    ).astype(BF16)


def pick_plan(columns, device, far, near):
    count = columns.shape[1]
    partner = columns[1:2, :]
    row = iota((1, count), 1).astype(F32)
    value = partner.astype(F32)
    perm = (iota((count, count), 0) == partner - device * count).astype(BF16)
    order = iota((PART, count), 0)
    send, take = [], []
    for other in (far, near):
        there = (partner >= other * count) & (partner < (other + 1) * count)
        for entry, found in ((row, send), (value, take)):
            first = jnp.min(jnp.where(there, entry, float(BIG)), axis=1, keepdims=True)
            last = jnp.max(jnp.where(there, entry, -1.0), axis=1, keepdims=True)
            wanted = jnp.where(order == 0, first, jnp.where(order == 1, last, -2.0))
            hit = jnp.where(there, entry, -3.0) == wanted
            found.append(hit.astype(F32).astype(BF16))
    return perm, jnp.concatenate(send, axis=0), jnp.concatenate(take, axis=0)


def kernel(
    a_hbm, t_ref, s_ref, col_ref, p_out, d_out, o_out,
    stage, ax, pn, yx, rr, pxl, other, pc, gath, below, above, xf, own, s32, plan_perm, plan_send,
    plan_take, snd, rcv, in_sem, out_sem, send_sem, recv_sem,
):
    device = lax.axis_index("rows")
    part = lax.axis_index("cols")
    devices = lax.axis_size("rows")
    parts = lax.axis_size("cols")
    far = lax.rem(device + devices // 2, devices)
    near = device + 1 - 2 * lax.rem(device, 2)
    up = lax.rem(device + 1, devices)
    down = lax.rem(device + devices - 1, devices)
    right = lax.rem(part + 1, parts)
    left = lax.rem(part + parts - 1, parts)
    opposite = lax.rem(part + 2, parts)

    def fetch(pair, slot):
        return pltpu.make_async_copy(a_hbm.at[pl.ds(2 * pair, 2)], stage.at[slot], in_sem.at[slot])

    def send(source, target, index, to):
        return pltpu.make_async_remote_copy(
            src_ref=source, dst_ref=target, send_sem=send_sem.at[index],
            recv_sem=recv_sem.at[index], device_id=to, device_id_type=MESH,
        )

    def exchange(turn):
        return [
            send(snd.at[turn, kind], rcv.at[turn, kind], 2 * turn + kind, (who, part))
            for kind, who in ((0, far), (1, near))
        ]

    fetch(0, 0).start()
    fetch(1, 1).start()
    barrier = pltpu.get_barrier_semaphore()
    for who in ((far, part), (up, part), (down, part), (device, right), (device, left)):
        pl.semaphore_signal(barrier, inc=1, device_id=who, device_id_type=MESH)

    perm, send_rows, take_rows = pick_plan(col_ref, device, far, near)
    plan_perm[...] = perm
    plan_send[...] = send_rows
    plan_take[...] = take_rows
    for half in range(2):
        s32[half] = s_ref[:, half * LAYER : (half + 1) * LAYER].astype(F32)

    def pack(turn, matrix):
        rows = lax.dot_general(plan_send[...], matrix, NT, preferred_element_type=F32).astype(BF16)
        snd[turn, 0] = rows[:PART]
        snd[turn, 1] = rows[PART:]

    def arrived(turn):
        rows = rcv[turn].reshape(2 * PART, -1)
        return lax.dot_general(rows, plan_take[...], TN, preferred_element_type=F32)

    pack(0, t_ref[...].reshape(BS * PART, 2 * LAYER))
    pl.semaphore_wait(barrier, 5)
    first = exchange(0)
    for copy in first:
        copy.start()

    fetch(0, 0).wait()
    relay(stage.at[0], ax.at[0])
    fetch(2, 0).start()

    for copy in first:
        copy.wait()
    moved = jnp.dot(
        t_ref[...].reshape(BS * PART, 2 * LAYER), plan_perm[...], preferred_element_type=F32
    )
    other[...] = (moved + arrived(0)).astype(BF16).reshape(BS, PART, 2 * LAYER)

    tt = ax.at[1, 0]
    cp = ax.at[1, 1]
    spread(lambda fine: [*halves(t_ref, fine), *halves(other, fine)] * 2, tt)

    lane = iota((1, 128), 1)
    mask = [((lane >= 32 * j) & (lane < 32 * j + 32)).astype(F32).astype(BF16) for j in range(4)]
    own_low = ((lane & 63) < 32).astype(F32).astype(BF16)
    own_high = ((lane & 63) >= 32).astype(F32).astype(BF16)
    first_layer = (iota((BS, 128), 1) & 16) == 0
    keep = ((iota((128, 128), 1) & 16) == 0) == (iota((128, 128), 0) < BS)

    def smooth(position):
        block = tt[of_position(position), :].astype(BF16)
        right_side = jnp.concatenate([block * own_low, block * own_high], axis=0)
        result = jnp.dot(left_of(ax, 0, position), right_side, preferred_element_type=F32)
        cp[of_position(position), :] = jnp.where(first_layer, result[:BS], result[BS:])

    loop(LAYER, 8, smooth)

    def back(pair):
        fine = 2 * pair
        joined = jnp.where(
            iota((LAYER, 128), 1) < 64, cp[group_rows(fine), :], cp[group_rows(fine + 1), :]
        ).T
        for step in range(2):
            for half in range(2):
                base = 64 * step + 16 * half
                coupled = joined[base : base + 16] + joined[base + 32 : base + 48]
                lanes = pl.ds(half * LAYER, LAYER)
                value = t_ref[fine + step, :, lanes].astype(F32)
                value = value - s32[half, pl.ds(fine + step, 1), :] * coupled
                value = value.astype(BF16)
                pxl[fine + step, :, lanes] = value
                rows = pl.ds(pl.multiple_of((fine + step) * PART, 8), PART)
                xf[half, rows, :] = value.astype(F32)

    loop(BS // 2, 4, back)

    def swap(coarse):
        for half in range(2):
            rows = xf[half, pl.ds(coarse, BS, stride=PART), :]
            pc[coarse, :, half * LAYER : (half + 1) * LAYER] = rows.astype(BF16)

    loop(PART, 4, swap)
    pack(1, pxl[...].reshape(BS * PART, 2 * LAYER))

    around = [
        send(pc, gath.at[0], 6, (device, right)),
        send(pc, gath.at[1], 7, (device, left)),
    ]
    halo = [
        send(pxl.at[:, :, pl.ds(LAYER, LAYER)], below, 8, (up, part)),
        send(pxl.at[:, :, pl.ds(0, LAYER)], above, 9, (down, part)),
    ]
    second = exchange(1)
    for copy in (*around, *halo, *second):
        copy.start()
    p_copy = pltpu.make_async_copy(pxl, p_out, out_sem.at[0])
    p_copy.start()

    spread(lambda fine: [*halves(pxl, fine)] * 4, yx)

    def settle(position):
        pn[position] = yx[of_position(position), :].astype(BF16)

    loop(LAYER, 8, settle)
    fetch(1, 1).wait()
    relay(stage.at[1], ax.at[1])
    fetch(3, 1).start()
    fetch(2, 0).wait()
    relay(stage.at[0], ax.at[2])

    def reach(slot, pairs, blocks, position):
        left_side = jnp.concatenate([left_of(ax, pair, position) for pair in pairs], axis=1)
        right_side = jnp.concatenate([block * m for block, m in zip(blocks, mask)], axis=0)
        result = jnp.dot(left_side, right_side, preferred_element_type=F32)
        rr[slot, position] = jnp.where(keep, result, 0.0).astype(BF16)

    def local_line(line, carry):
        before = lax.rem(line + GY - 1, GY) * GX
        after = lax.rem(line + 1, GY) * GX
        base = line * GX
        for x in range(GX):
            blocks = [
                pn[base + (x + GX - 1) % GX], pn[base + (x + 1) % GX], pn[before + x], pn[after + x]
            ]
            reach(0, (1, 2), blocks, base + x)
        return carry

    lax.fori_loop(0, GY, local_line, 0)

    for copy in around:
        copy.wait()
    middle = PART // 2
    relays = [
        send(gath.at[0, pl.ds(0, middle)], gath.at[2, pl.ds(0, middle)], 10, (device, right)),
        send(
            gath.at[1, pl.ds(middle, middle)], gath.at[2, pl.ds(middle, middle)], 11, (device, left)
        ),
    ]
    for copy in relays:
        copy.start()

    fetch(3, 1).wait()
    relay(stage.at[1], ax.at[1])
    for copy in second:
        copy.wait()
    moved = jnp.dot(
        pxl[...].reshape(BS * PART, 2 * LAYER), plan_perm[...], preferred_element_type=F32
    )
    other[...] = (moved + arrived(1)).astype(BF16).reshape(BS, PART, 2 * LAYER)
    for copy in halo:
        copy.wait()

    def outer_rows(fine):
        low, high = halves(pxl, fine)
        return [low, high, *halves(other, fine), below[fine], low, high, above[fine]]

    spread(outer_rows, yx)

    def remote_row(position):
        block = yx[of_position(position), :].astype(BF16)
        reach(1, (0, 1), [block] * 4, position)

    loop(LAYER, 8, remote_row)

    pf = ax.at[2, 0]

    def wide(source, index, owner):
        def body(coarse):
            block = source[coarse] if index is None else source[index, coarse]
            rows = jnp.concatenate([block[:, :LAYER], block[:, LAYER:]], axis=0)
            pf[group_rows(owner * PART + coarse), :] = rows.T.astype(F32)

        loop(PART, 8, body)

    wide(pc, None, part)
    wide(gath, 0, left)
    wide(gath, 1, right)
    for copy in relays:
        copy.wait()
    wide(gath, 2, opposite)

    def product(position):
        left_side = pf[of_position(position), :].astype(BF16)
        right_side = jnp.concatenate([rr[0, position], rr[1, position]], axis=1)
        result = jnp.dot(left_side, right_side, preferred_element_type=F32)
        for slot in range(2):
            ax[0, slot, of_position(position), :] = result[:, slot * 128 : (slot + 1) * 128]

    loop(LAYER, 8, product)

    def keep_off(slot, half, coarse_row, rows):
        start = slot * BS + coarse_row
        ax[1, half, pl.ds(start, PART, stride=CSTRIDE), :] = rows

    def finish_outer(coarse_row):
        turned = ax[0, 1, group_rows(coarse_row), :].T
        for half in range(2):
            rows = [turned[32 * j + 16 * half : 32 * j + 16 * half + 16] for j in range(4)]
            own[half, pl.ds(coarse_row, PART, stride=BS), :] = rows[0] + rows[1]
            keep_off(4, half, coarse_row, rows[2])
            keep_off(5, half, coarse_row, rows[3])

    loop(BS, 4, finish_outer)

    high = jnp.concatenate([own[0], own[1]], axis=1).astype(BF16)
    pack(2, high)
    third = exchange(2)
    for copy in third:
        copy.start()

    def finish_local(coarse_row):
        turned = ax[0, 0, group_rows(coarse_row), :].T
        for half in range(2):
            for j in range(4):
                keep_off(j, half, coarse_row, turned[32 * j + 16 * half : 32 * j + 16 * half + 16])

    loop(BS, 4, finish_local)

    def narrow(coarse):
        for slot in range(6):
            for half in range(2):
                start = pl.multiple_of(coarse * CSTRIDE + slot * BS, 8)
                plane = coarse * 6 + slot
                stage[0, plane // BS, lax.rem(plane, BS), :, half * LAYER : (half + 1) * LAYER] = ax[
                    1, half, pl.ds(start, BS), :
                ].astype(BF16)

    loop(PART, 1, narrow)
    o_copies = [
        pltpu.make_async_copy(stage.at[0, 0], o_out.at[pl.ds(0, BS)], out_sem.at[1]),
        pltpu.make_async_copy(
            stage.at[0, 1, pl.ds(0, 6 * PART - BS)], o_out.at[pl.ds(BS, 6 * PART - BS)], out_sem.at[2]
        ),
    ]
    for copy in o_copies:
        copy.start()

    whole = jnp.concatenate([own[0], own[1]], axis=1)
    high = whole.astype(BF16)
    low = (whole - high.astype(F32)).astype(BF16)
    total = whole + jnp.dot(high, plan_perm[...], preferred_element_type=F32)
    total = total + jnp.dot(low, plan_perm[...], preferred_element_type=F32)
    for copy in third:
        copy.wait()
    total = total + arrived(2)
    for half in range(2):
        own[half] = total[:, half * LAYER : (half + 1) * LAYER]
    d_copies = [
        pltpu.make_async_copy(own.at[half], d_out.at[:, pl.ds(half * LAYER, LAYER)], out_sem.at[3 + half])
        for half in range(2)
    ]
    for copy in d_copies:
        copy.start()
    for copy in (p_copy, *o_copies, *d_copies):
        copy.wait()


def on_device(operator_blocks, tentative, jacobi_scale, columns):
    rows = columns.shape[1]
    vmem = pl.BlockSpec(memory_space=pltpu.VMEM)
    hbm = pl.BlockSpec(memory_space=pl.ANY)
    prolongator, diag, off = pl.pallas_call(
        kernel,
        out_shape=(
            jax.ShapeDtypeStruct((BS, PART, rows), BF16),
            jax.ShapeDtypeStruct((PART * BS, rows), F32),
            jax.ShapeDtypeStruct((PART * 6, BS, rows), BF16),
        ),
        in_specs=[hbm, vmem, vmem, vmem],
        out_specs=(hbm, hbm, hbm),
        scratch_shapes=[
            pltpu.VMEM((2, 2, BS, BS, rows), BF16),
            pltpu.VMEM((3, 2, BS * STRIDE, 128), F32),
            pltpu.VMEM((LAYER, BS, 128), BF16),
            pltpu.VMEM((BS * STRIDE, 128), F32),
            pltpu.VMEM((2, LAYER, 128, 128), BF16),
            pltpu.VMEM((BS, PART, rows), BF16),
            pltpu.VMEM((BS, PART, rows), BF16),
            pltpu.VMEM((PART, BS, rows), BF16),
            pltpu.VMEM((3, PART, BS, rows), BF16),
            pltpu.VMEM((BS, PART, LAYER), BF16),
            pltpu.VMEM((BS, PART, LAYER), BF16),
            pltpu.VMEM((2, BS * PART, LAYER), F32),
            pltpu.VMEM((2, BS * PART, LAYER), F32),
            pltpu.VMEM((2, BS, LAYER), F32),
            pltpu.VMEM((rows, rows), BF16),
            pltpu.VMEM((2 * PART, rows), BF16),
            pltpu.VMEM((2 * PART, rows), BF16),
            pltpu.VMEM((3, 2, PART, BS * PART), BF16),
            pltpu.VMEM((3, 2, PART, BS * PART), BF16),
            pltpu.SemaphoreType.DMA((2,)),
            pltpu.SemaphoreType.DMA((5,)),
            pltpu.SemaphoreType.DMA((12,)),
            pltpu.SemaphoreType.DMA((12,)),
        ],
        compiler_params=pltpu.CompilerParams(
            collective_id=0, has_side_effects=True, vmem_limit_bytes=60 * 2**20
        ),
    )(operator_blocks, tentative, jacobi_scale, columns)
    return prolongator, diag.reshape(PART, BS, rows), off.reshape(PART, 6, BS, rows)


def solution(mesh):
    placed = (
        P(None, None, None, "rows"),
        P(None, "cols", "rows"),
        P(None, "rows"),
        P(None, "rows"),
    )
    return jax.shard_map(
        on_device,
        mesh=mesh,
        in_specs=placed,
        out_specs=(P(None, "cols", "rows"), P("cols", None, "rows"), P("cols", None, None, "rows")),
        check_vma=False,
    )
```

time: 243 us -> 67.4 us (0.28); the launches traced: 240 us -> 67.2 us
  local copies, waits for them, and re-layouts: 139 us -> 5.98 us
  Pallas kernels: 0 us -> 60.6 us
  starting transfers between devices: 39.1 us -> 0 us
  matrix products: 35 us -> 0 us
  waiting for transfers between devices: 14.3 us -> 0 us
  other arithmetic: 12.1 us -> 0 us
    unnamed x24 -> x5, local copies, waits for them, and re-layouts: 76.3 us -> 5.98 us
    pallas_call x0 -> x1, Pallas kernels: none -> 60.6 us  [on_device(): pl.pallas_call(kernel, out_shape=(jax.ShapeDtypeStruct((BS, PART, rows),...]
    all_to_all x4 -> x0, starting transfers between devices: 35.2 us -> none  [the longest x1 12.1 us: on_device(): lax.all_to_all(pack_rows(tentative, send_slots, devices), 'rows', split_a...]
    dot_general x3 -> x0, matrix products: 35 us -> none  [the longest x1 28.1 us: coarse_terms(): jnp.einsum('fax,kfcx->ckax', left_full, reached, preferred_element_type=j...]
    gather x10 -> x0, local copies, waits for them, and re-layouts: 26.1 us -> none  [the longest x1 16.2 us: on_device(): jnp.take(source, positions.reshape(-1), axis=2)]
    slice x4 -> x0, local copies, waits for them, and re-layouts: 13.6 us -> none  [the longest x1 8.71 us: on_device(): coarse_off = contributions[:, 2:].astype(jnp.bfloat16)]
    reshape x10 -> x0, local copies, waits for them, and re-layouts: 13.5 us -> none  [the longest x1 6.67 us: laid_out(): parts.reshape(*lengths[:dim], lengths[dim] * lengths[dim + 1], *lengths[d...]
    all_to_all x4 -> x0, waiting for transfers between devices: 11.3 us -> none  [the longest x1 11.3 us: on_device(): lax.all_to_all(pack_rows(prolongator, send_slots, devices), 'rows', split...]
  transfers between devices with their start and end apart: 6 -> 0, of which waited for: 2 -> 0; matrix products, arithmetic and copies ran while one was open for 44% -> 0% of each run, Pallas kernels for 0% -> 0%
where the time goes in v1:
time: 67.4 us; the launch traced here: 67.2 us
  Pallas kernels  60.6 us (90%)
  local copies, waits for them, and re-layouts  5.98 us (9%)
    pallas_call x1, Pallas kernels, on_device(): pl.pallas_call(kernel, out_shape=(jax.ShapeDtypeStruct((BS, PART, rows),...  60.6 us
    unnamed x5, local copies, waits for them, and re-layouts  5.98 us

profile of v1, /device:TPU:4, one launch (start us, length us, event | category | flops | bytes accessed | tf_op | source)
XLA Modules:
  0.0 67.2 jit_solution(373393621137590166)
XLA Ops:
  0.6 60.6 %shard_map.67 = (bf16[64,16,256]{2,1,0:T(8,128)(2,1)}, f32[1024,256]{1,0:T(8,128)}, bf16[96,64,256]{2,1,0:T(8,128)(2,1)}) custom-call(bf16[8,64,64,256]{3,2,1,0:T(8,128)(2,1)} %a_hbm.1, bf16[64,16,256]{2,1,0:T(8,128)(2,1)} %t_ref.1, bf16[64,256]{1,0:T(8,128)(2,1)} %s_ref.1, s32[8,256]{1,0:T(8,128)} %col_ref.1), custom_call_target="tpu_custom_call" | custom-call | tf_op jit(solution)/shard_map/pallas_call | solution.py:385
  61.2 0.0 copy-start
  61.3 2.0 %copy.10 = bf16[64,16,256]{2,1,0:T(8,128)(2,1)} copy(bf16[64,16,256]{2,1,0:T(8,128)(2,1)} %get-tuple-element.12) | data formatting | bytes 1048576
  63.3 2.3 %copy.11 = f32[16,64,256]{2,1,0:T(8,128)} copy(f32[16,64,256]{2,1,0:T(8,128)} %bitcast.3) | data formatting | bytes 2097152
  65.6 0.0 copy-done
  65.6 1.7 %copy.12 = bf16[16,6,64,256]{3,2,1,0:T(8,128)(2,1)} copy(bf16[16,6,64,256]{3,2,1,0:T(8,128)(2,1)S(1)} %bitcast.2) | data formatting | bytes 6291456
Async XLA Ops:
  61.2 4.3 %copy-start = (bf16[96,64,256]{2,1,0:T(8,128)(2,1)S(1)}, bf16[96,64,256]{2,1,0:T(8,128)(2,1)}, u32[]{:S(2)}) copy-start(bf16[96,64,256]{2,1,0:T(8,128)(2,1)} %get-tuple-element.8) | copy-start | bytes 9437188

commit v2 on v1

--- a/solution.py
+++ b/solution.py
@@ -12,8 +12,10 @@
 LAYER = GX * GY
 BS = 64
 PART = 16
-STRIDE = LAYER + 8
-CSTRIDE = 392
+STRIDE = LAYER + 4
+CSTRIDE = 388
+OSTRIDE = BS + 4
+XSTRIDE = PART + 4
 BIG = 1 << 20
 MESH = pl.DeviceIdType.MESH
 F32 = jnp.float32
@@ -27,7 +29,7 @@
 
 
 def group_rows(block):
-    return pl.ds(pl.multiple_of(block * STRIDE, 8), LAYER)
+    return pl.ds(block * STRIDE, LAYER)
 
 
 def of_position(position):
@@ -43,13 +45,14 @@
     lax.fori_loop(0, count // unroll, step, 0)
 
 
-def relay(stage, target):
-    def body(fine):
-        for half in range(2):
-            block = stage[:, fine, :, half * LAYER : (half + 1) * LAYER].reshape(128, LAYER)
-            target[half, group_rows(fine), :] = block.T.astype(F32)
-
-    loop(BS, 8, body)
+def relay_one(stage, targets, fine):
+    for half in range(2):
+        block = stage[:, fine, :, half * LAYER : (half + 1) * LAYER].reshape(128, LAYER)
+        targets[half][group_rows(fine), :] = block.T.astype(F32)
+
+
+def relay(stage, targets):
+    loop(BS, 8, lambda fine: relay_one(stage, targets, fine))
 
 
 def spread(rows_of, target):
@@ -63,9 +66,9 @@
     return ref[index, :, :LAYER], ref[index, :, LAYER:]
 
 
-def left_of(ax, pair, position):
+def left_of(sources, position):
     return jnp.concatenate(
-        [ax[pair, half, of_position(position), :] for half in range(2)], axis=0
+        [source[of_position(position), :] for source in sources], axis=0
     ).astype(BF16)
 
 
@@ -89,9 +92,9 @@
 
 
 def kernel(
-    a_hbm, t_ref, s_ref, col_ref, p_out, d_out, o_out,
-    stage, ax, pn, yx, rr, pxl, other, pc, gath, below, above, xf, own, s32, plan_perm, plan_send,
-    plan_take, snd, rcv, in_sem, out_sem, send_sem, recv_sem,
+    a_hbm, t_ref, s_ref, col_ref, pxl, xf, b2, b3,
+    stage, b0, b1, b4, b5, b6, pn, yx, rr, other, pc, gath, below, above, own, s32, plan_perm, plan_send,
+    plan_take, snd, rcv, in_sem, chunk_sem, send_sem, recv_sem,
 ):
     device = lax.axis_index("rows")
     part = lax.axis_index("cols")
@@ -120,7 +123,14 @@
             for kind, who in ((0, far), (1, near))
         ]
 
-    fetch(0, 0).start()
+    def first_fetch(chunk):
+        rows = pl.ds(chunk * 16, 16)
+        return pltpu.make_async_copy(
+            a_hbm.at[pl.ds(0, 2), rows], stage.at[0, :, rows], chunk_sem.at[chunk]
+        )
+
+    for chunk in range(4):
+        first_fetch(chunk).start()
     fetch(1, 1).start()
     barrier = pltpu.get_barrier_semaphore()
     for who in ((far, part), (up, part), (down, part), (device, right), (device, left)):
@@ -148,8 +158,9 @@
     for copy in first:
         copy.start()
 
-    fetch(0, 0).wait()
-    relay(stage.at[0], ax.at[0])
+    for chunk in range(4):
+        first_fetch(chunk).wait()
+        loop(16, 8, lambda fine: relay_one(stage.at[0], (b0, b1), 16 * chunk + fine))
     fetch(2, 0).start()
 
     for copy in first:
@@ -159,8 +170,7 @@
     )
     other[...] = (moved + arrived(0)).astype(BF16).reshape(BS, PART, 2 * LAYER)
 
-    tt = ax.at[1, 0]
-    cp = ax.at[1, 1]
+    tt, cp = yx, b6
     spread(lambda fine: [*halves(t_ref, fine), *halves(other, fine)] * 2, tt)
 
     lane = iota((1, 128), 1)
@@ -173,7 +183,7 @@
     def smooth(position):
         block = tt[of_position(position), :].astype(BF16)
         right_side = jnp.concatenate([block * own_low, block * own_high], axis=0)
-        result = jnp.dot(left_of(ax, 0, position), right_side, preferred_element_type=F32)
+        result = jnp.dot(left_of((b0, b1), position), right_side, preferred_element_type=F32)
         cp[of_position(position), :] = jnp.where(first_layer, result[:BS], result[BS:])
 
     loop(LAYER, 8, smooth)
@@ -192,32 +202,41 @@
                 value = value - s32[half, pl.ds(fine + step, 1), :] * coupled
                 value = value.astype(BF16)
                 pxl[fine + step, :, lanes] = value
-                rows = pl.ds(pl.multiple_of((fine + step) * PART, 8), PART)
+                rows = pl.ds((fine + step) * XSTRIDE, PART)
                 xf[half, rows, :] = value.astype(F32)
 
     loop(BS // 2, 4, back)
 
     def swap(coarse):
         for half in range(2):
-            rows = xf[half, pl.ds(coarse, BS, stride=PART), :]
+            rows = xf[half, pl.ds(coarse, BS, stride=XSTRIDE), :]
             pc[coarse, :, half * LAYER : (half + 1) * LAYER] = rows.astype(BF16)
 
     loop(PART, 4, swap)
     pack(1, pxl[...].reshape(BS * PART, 2 * LAYER))
 
-    around = [
-        send(pc, gath.at[0], 6, (device, right)),
-        send(pc, gath.at[1], 7, (device, left)),
+    middle = PART // 2
+    low = pl.ds(0, middle)
+    high = pl.ds(middle, middle)
+    first_half = [
+        send(pc.at[low], gath.at[0, low], 6, (device, right)),
+        send(pc.at[high], gath.at[1, high], 7, (device, left)),
+    ]
+    second_half = [
+        send(pc.at[high], gath.at[0, high], 12, (device, right)),
+        send(pc.at[low], gath.at[1, low], 13, (device, left)),
+    ]
+    relays = [
+        send(gath.at[0, low], gath.at[2, low], 10, (device, right)),
+        send(gath.at[1, high], gath.at[2, high], 11, (device, left)),
     ]
     halo = [
         send(pxl.at[:, :, pl.ds(LAYER, LAYER)], below, 8, (up, part)),
         send(pxl.at[:, :, pl.ds(0, LAYER)], above, 9, (down, part)),
     ]
     second = exchange(1)
-    for copy in (*around, *halo, *second):
+    for copy in (*second, *first_half, *halo, *second_half):
         copy.start()
-    p_copy = pltpu.make_async_copy(pxl, p_out, out_sem.at[0])
-    p_copy.start()
 
     spread(lambda fine: [*halves(pxl, fine)] * 4, yx)
 
@@ -226,13 +245,18 @@
 
     loop(LAYER, 8, settle)
     fetch(1, 1).wait()
-    relay(stage.at[1], ax.at[1])
+    relay(stage.at[1], (b2, b3))
     fetch(3, 1).start()
     fetch(2, 0).wait()
-    relay(stage.at[0], ax.at[2])
+    relay(stage.at[0], (b4, b5))
+    for copy in first_half:
+        copy.wait_recv()
+    for copy in relays:
+        copy.start()
+    fetch(3, 1).wait()
 
     def reach(slot, pairs, blocks, position):
-        left_side = jnp.concatenate([left_of(ax, pair, position) for pair in pairs], axis=1)
+        left_side = jnp.concatenate([left_of(pair, position) for pair in pairs], axis=1)
         right_side = jnp.concatenate([block * m for block, m in zip(blocks, mask)], axis=0)
         result = jnp.dot(left_side, right_side, preferred_element_type=F32)
         rr[slot, position] = jnp.where(keep, result, 0.0).astype(BF16)
@@ -245,25 +269,13 @@
             blocks = [
                 pn[base + (x + GX - 1) % GX], pn[base + (x + 1) % GX], pn[before + x], pn[after + x]
             ]
-            reach(0, (1, 2), blocks, base + x)
+            reach(0, ((b2, b3), (b4, b5)), blocks, base + x)
+        for inner in range(4):
+            relay_one(stage.at[1], (b6, yx), line * 4 + inner)
         return carry
 
     lax.fori_loop(0, GY, local_line, 0)
 
-    for copy in around:
-        copy.wait()
-    middle = PART // 2
-    relays = [
-        send(gath.at[0, pl.ds(0, middle)], gath.at[2, pl.ds(0, middle)], 10, (device, right)),
-        send(
-            gath.at[1, pl.ds(middle, middle)], gath.at[2, pl.ds(middle, middle)], 11, (device, left)
-        ),
-    ]
-    for copy in relays:
-        copy.start()
-
-    fetch(3, 1).wait()
-    relay(stage.at[1], ax.at[1])
     for copy in second:
         copy.wait()
     moved = jnp.dot(
@@ -277,15 +289,15 @@
         low, high = halves(pxl, fine)
         return [low, high, *halves(other, fine), below[fine], low, high, above[fine]]
 
-    spread(outer_rows, yx)
+    spread(outer_rows, b2)
 
     def remote_row(position):
-        block = yx[of_position(position), :].astype(BF16)
-        reach(1, (0, 1), [block] * 4, position)
+        block = b2[of_position(position), :].astype(BF16)
+        reach(1, ((b0, b1), (b6, yx)), [block] * 4, position)
 
     loop(LAYER, 8, remote_row)
 
-    pf = ax.at[2, 0]
+    pf, off = b4, (b2, b3)
 
     def wide(source, index, owner):
         def body(coarse):
@@ -296,6 +308,10 @@
         loop(PART, 8, body)
 
     wide(pc, None, part)
+    for copy in first_half:
+        copy.wait_send()
+    for copy in second_half:
+        copy.wait()
     wide(gath, 0, left)
     wide(gath, 1, right)
     for copy in relays:
@@ -306,59 +322,57 @@
         left_side = pf[of_position(position), :].astype(BF16)
         right_side = jnp.concatenate([rr[0, position], rr[1, position]], axis=1)
         result = jnp.dot(left_side, right_side, preferred_element_type=F32)
-        for slot in range(2):
-            ax[0, slot, of_position(position), :] = result[:, slot * 128 : (slot + 1) * 128]
+        b0[of_position(position), :] = result[:, :128]
+        b1[of_position(position), :] = result[:, 128:]
 
     loop(LAYER, 8, product)
 
     def keep_off(slot, half, coarse_row, rows):
         start = slot * BS + coarse_row
-        ax[1, half, pl.ds(start, PART, stride=CSTRIDE), :] = rows
+        off[half][pl.ds(start, PART, stride=CSTRIDE), :] = rows
 
     def finish_outer(coarse_row):
-        turned = ax[0, 1, group_rows(coarse_row), :].T
+        block = b1[group_rows(coarse_row), :]
+        high = block.astype(BF16)
+        low = (block - high.astype(F32)).astype(BF16)
+        turned = high.T.astype(F32)
+        fixed = turned[:64] + low.T[:64].astype(F32)
         for half in range(2):
             rows = [turned[32 * j + 16 * half : 32 * j + 16 * half + 16] for j in range(4)]
-            own[half, pl.ds(coarse_row, PART, stride=BS), :] = rows[0] + rows[1]
+            own[half, pl.ds(coarse_row, PART, stride=OSTRIDE), :] = (
+                fixed[16 * half : 16 * half + 16] + fixed[32 + 16 * half : 48 + 16 * half]
+            )
             keep_off(4, half, coarse_row, rows[2])
             keep_off(5, half, coarse_row, rows[3])
 
     loop(BS, 4, finish_outer)
 
-    high = jnp.concatenate([own[0], own[1]], axis=1).astype(BF16)
+    def own_rows():
+        return jnp.concatenate(
+            [
+                jnp.concatenate(
+                    [own[half, pl.ds(c * OSTRIDE, BS), :] for c in range(PART)], axis=0
+                )
+                for half in range(2)
+            ],
+            axis=1,
+        )
+
+    high = own_rows().astype(BF16)
     pack(2, high)
     third = exchange(2)
     for copy in third:
         copy.start()
 
     def finish_local(coarse_row):
-        turned = ax[0, 0, group_rows(coarse_row), :].T
+        turned = b0[group_rows(coarse_row), :].astype(BF16).T.astype(F32)
         for half in range(2):
             for j in range(4):
                 keep_off(j, half, coarse_row, turned[32 * j + 16 * half : 32 * j + 16 * half + 16])
 
     loop(BS, 4, finish_local)
 
-    def narrow(coarse):
-        for slot in range(6):
-            for half in range(2):
-                start = pl.multiple_of(coarse * CSTRIDE + slot * BS, 8)
-                plane = coarse * 6 + slot
-                stage[0, plane // BS, lax.rem(plane, BS), :, half * LAYER : (half + 1) * LAYER] = ax[
-                    1, half, pl.ds(start, BS), :
-                ].astype(BF16)
-
-    loop(PART, 1, narrow)
-    o_copies = [
-        pltpu.make_async_copy(stage.at[0, 0], o_out.at[pl.ds(0, BS)], out_sem.at[1]),
-        pltpu.make_async_copy(
-            stage.at[0, 1, pl.ds(0, 6 * PART - BS)], o_out.at[pl.ds(BS, 6 * PART - BS)], out_sem.at[2]
-        ),
-    ]
-    for copy in o_copies:
-        copy.start()
-
-    whole = jnp.concatenate([own[0], own[1]], axis=1)
+    whole = own_rows()
     high = whole.astype(BF16)
     low = (whole - high.astype(F32)).astype(BF16)
     total = whole + jnp.dot(high, plan_perm[...], preferred_element_type=F32)
@@ -367,14 +381,35 @@
         copy.wait()
     total = total + arrived(2)
     for half in range(2):
-        own[half] = total[:, half * LAYER : (half + 1) * LAYER]
-    d_copies = [
-        pltpu.make_async_copy(own.at[half], d_out.at[:, pl.ds(half * LAYER, LAYER)], out_sem.at[3 + half])
+        xf[half, pl.ds(0, PART * BS), :] = total[:, half * LAYER : (half + 1) * LAYER]
+
+
+def finish(p_ref, d_ref, low_ref, high_ref, p_out, d_out, o_out, planes, sems):
+    early = [pltpu.make_async_copy(p_ref, p_out, sems.at[0])] + [
+        pltpu.make_async_copy(
+            d_ref.at[half, pl.ds(0, PART * BS)],
+            d_out.at[:, pl.ds(half * LAYER, LAYER)],
+            sems.at[1 + half],
+        )
         for half in range(2)
     ]
-    for copy in d_copies:
+    for copy in early:
         copy.start()
-    for copy in (p_copy, *o_copies, *d_copies):
+    late = []
+    for chunk in range(4):
+
+        def narrow(step):
+            coarse = 4 * chunk + step
+            for slot in range(6):
+                for half, source in enumerate((low_ref, high_ref)):
+                    rows = source[pl.ds(coarse * CSTRIDE + slot * BS, BS), :]
+                    planes[coarse * 6 + slot, :, half * LAYER : (half + 1) * LAYER] = rows.astype(BF16)
+
+        loop(4, 1, narrow)
+        there = pl.ds(24 * chunk, 24)
+        late.append(pltpu.make_async_copy(planes.at[there], o_out.at[there], sems.at[3 + chunk]))
+        late[-1].start()
+    for copy in (*early, *late):
         copy.wait()
 
 
@@ -382,29 +417,28 @@
     rows = columns.shape[1]
     vmem = pl.BlockSpec(memory_space=pltpu.VMEM)
     hbm = pl.BlockSpec(memory_space=pl.ANY)
-    prolongator, diag, off = pl.pallas_call(
+    kept = pl.pallas_call(
         kernel,
         out_shape=(
-            jax.ShapeDtypeStruct((BS, PART, rows), BF16),
-            jax.ShapeDtypeStruct((PART * BS, rows), F32),
-            jax.ShapeDtypeStruct((PART * 6, BS, rows), BF16),
+            pltpu.VMEM((BS, PART, rows), BF16),
+            pltpu.VMEM((2, BS * XSTRIDE, LAYER), F32),
+            pltpu.VMEM((BS * STRIDE, 128), F32),
+            pltpu.VMEM((BS * STRIDE, 128), F32),
         ),
         in_specs=[hbm, vmem, vmem, vmem],
-        out_specs=(hbm, hbm, hbm),
+        out_specs=(vmem,) * 4,
         scratch_shapes=[
             pltpu.VMEM((2, 2, BS, BS, rows), BF16),
-            pltpu.VMEM((3, 2, BS * STRIDE, 128), F32),
+            *[pltpu.VMEM((BS * STRIDE, 128), F32) for _ in range(5)],
             pltpu.VMEM((LAYER, BS, 128), BF16),
             pltpu.VMEM((BS * STRIDE, 128), F32),
             pltpu.VMEM((2, LAYER, 128, 128), BF16),
-            pltpu.VMEM((BS, PART, rows), BF16),
             pltpu.VMEM((BS, PART, rows), BF16),
             pltpu.VMEM((PART, BS, rows), BF16),
             pltpu.VMEM((3, PART, BS, rows), BF16),
             pltpu.VMEM((BS, PART, LAYER), BF16),
             pltpu.VMEM((BS, PART, LAYER), BF16),
-            pltpu.VMEM((2, BS * PART, LAYER), F32),
-            pltpu.VMEM((2, BS * PART, LAYER), F32),
+            pltpu.VMEM((2, PART * OSTRIDE, LAYER), F32),
             pltpu.VMEM((2, BS, LAYER), F32),
             pltpu.VMEM((rows, rows), BF16),
             pltpu.VMEM((2 * PART, rows), BF16),
@@ -412,14 +446,29 @@
             pltpu.VMEM((3, 2, PART, BS * PART), BF16),
             pltpu.VMEM((3, 2, PART, BS * PART), BF16),
             pltpu.SemaphoreType.DMA((2,)),
-            pltpu.SemaphoreType.DMA((5,)),
-            pltpu.SemaphoreType.DMA((12,)),
-            pltpu.SemaphoreType.DMA((12,)),
+            pltpu.SemaphoreType.DMA((4,)),
+            pltpu.SemaphoreType.DMA((14,)),
+            pltpu.SemaphoreType.DMA((14,)),
         ],
         compiler_params=pltpu.CompilerParams(
-            collective_id=0, has_side_effects=True, vmem_limit_bytes=60 * 2**20
+            collective_id=0, has_side_effects=True, vmem_limit_bytes=51 * 2**20
         ),
     )(operator_blocks, tentative, jacobi_scale, columns)
+    prolongator, diag, off = pl.pallas_call(
+        finish,
+        out_shape=(
+            jax.ShapeDtypeStruct((BS, PART, rows), BF16),
+            jax.ShapeDtypeStruct((PART * BS, rows), F32),
+            jax.ShapeDtypeStruct((PART * 6, BS, rows), BF16),
+        ),
+        in_specs=[vmem] * 4,
+        out_specs=(hbm,) * 3,
+        scratch_shapes=[
+            pltpu.VMEM((PART * 6, BS, rows), BF16),
+            pltpu.SemaphoreType.DMA((7,)),
+        ],
+        compiler_params=pltpu.CompilerParams(vmem_limit_bytes=8 * 2**20),
+    )(*kept)
     return prolongator, diag.reshape(PART, BS, rows), off.reshape(PART, 6, BS, rows)
 
 

time: 67.4 us -> 52.6 us (0.78); the launches traced: 67.2 us -> 51.7 us
  Pallas kernels: 60.6 us -> 51.1 us
  local copies, waits for them, and re-layouts: 5.98 us -> 0 us
    pallas_call x1 -> x2, Pallas kernels: 60.6 us -> 51.1 us  [the longest x1 48.8 us: on_device(): pl.pallas_call(kernel, out_shape=(pltpu.VMEM((BS, PART, rows), BF16), plt...]
    unnamed x5 -> x0, local copies, waits for them, and re-layouts: 5.98 us -> none
where the time goes in v2:
time: 52.6 us; the launch traced here: 51.7 us
  Pallas kernels  51.1 us (97%)
  between operations  0.64 us (1%)
    pallas_call x1, Pallas kernels, on_device(): pl.pallas_call(kernel, out_shape=(pltpu.VMEM((BS, PART, rows), BF16), plt...  48.8 us
    pallas_call x1, Pallas kernels, on_device(): pl.pallas_call(finish, out_shape=(jax.ShapeDtypeStruct((BS, PART, rows),...  2.24 us

profile of v2, /device:TPU:4, one launch (start us, length us, event | category | flops | bytes accessed | tf_op | source)
XLA Modules:
  0.0 51.7 jit_solution(14215906772683351938)
XLA Ops:
  0.6 48.8 %shard_map.67 = (bf16[64,16,256]{2,1,0:T(8,128)(2,1)S(1)}, f32[2,1280,128]{2,1,0:T(8,128)S(1)}, f32[8448,128]{1,0:T(8,128)S(1)}, f32[8448,128]{1,0:T(8,128)S(1)}) custom-call(bf16[8,64,64,256]{3,2,1,0:T(8,128)(2,1)} %a_hbm.1, bf16[64,16,256]{2,1,0:T(8,128)(2,1)} %t_ref.1, bf16[64,256]{1,0:T(8,128)(2,1)} %s_ref.1, s32[8,256]{1,0:T(8,128)} %col_ref.1), custom_call_target="tpu_custom_call" | custom-call | tf_op jit(solution)/shard_map/pallas_call | solution.py:420
  49.5 2.2 %shard_map.68 = (bf16[64,16,256]{2,1,0:T(8,128)(2,1)}, f32[1024,256]{1,0:T(8,128)}, bf16[96,64,256]{2,1,0:T(8,128)(2,1)}) custom-call(bf16[64,16,256]{2,1,0:T(8,128)(2,1)S(1)} %get-tuple-element.10.p_ref, f32[2,1280,128]{2,1,0:T(8,128)S(1)} %get-tuple-element.11.d_ref, f32[8448,128]{1,0:T(8,128)S(1)} %get-tuple-element.12.low_ref, ...), custom_call_target="tpu_custom_call" | custom-call | tf_op jit(solution)/shard_map/pallas_call | solution.py:457

commit v3 on v2

--- a/solution.py
+++ b/solution.py
@@ -59,7 +59,7 @@
     def body(fine):
         target[group_rows(fine), :] = jnp.concatenate(rows_of(fine), axis=0).T.astype(F32)
 
-    loop(BS, 8, body)
+    loop(BS, 16, body)
 
 
 def halves(ref, index):
@@ -163,6 +163,9 @@
         loop(16, 8, lambda fine: relay_one(stage.at[0], (b0, b1), 16 * chunk + fine))
     fetch(2, 0).start()
 
+    fetch(1, 1).wait()
+    relay(stage.at[1], (b2, b3))
+    fetch(3, 1).start()
     for copy in first:
         copy.wait()
     moved = jnp.dot(
@@ -186,7 +189,7 @@
         result = jnp.dot(left_of((b0, b1), position), right_side, preferred_element_type=F32)
         cp[of_position(position), :] = jnp.where(first_layer, result[:BS], result[BS:])
 
-    loop(LAYER, 8, smooth)
+    loop(LAYER, 32, smooth)
 
     def back(pair):
         fine = 2 * pair
@@ -244,9 +247,6 @@
         pn[position] = yx[of_position(position), :].astype(BF16)
 
     loop(LAYER, 8, settle)
-    fetch(1, 1).wait()
-    relay(stage.at[1], (b2, b3))
-    fetch(3, 1).start()
     fetch(2, 0).wait()
     relay(stage.at[0], (b4, b5))
     for copy in first_half:
@@ -274,7 +274,10 @@
             relay_one(stage.at[1], (b6, yx), line * 4 + inner)
         return carry
 
-    lax.fori_loop(0, GY, local_line, 0)
+    def two_lines(index, carry):
+        return local_line(2 * index + 1, local_line(2 * index, carry))
+
+    lax.fori_loop(0, GY // 2, two_lines, 0)
 
     for copy in second:
         copy.wait()
@@ -295,57 +298,69 @@
         block = b2[of_position(position), :].astype(BF16)
         reach(1, ((b0, b1), (b6, yx)), [block] * 4, position)
 
-    loop(LAYER, 8, remote_row)
+    loop(LAYER, 32, remote_row)
 
     pf, off = b4, (b2, b3)
 
-    def wide(source, index, owner):
+    def wide(source, index, place):
         def body(coarse):
             block = source[coarse] if index is None else source[index, coarse]
             rows = jnp.concatenate([block[:, :LAYER], block[:, LAYER:]], axis=0)
-            pf[group_rows(owner * PART + coarse), :] = rows.T.astype(F32)
-
-        loop(PART, 8, body)
-
-    wide(pc, None, part)
+            pf[group_rows(place * PART + coarse), :] = rows.T.astype(F32)
+
+        loop(PART, 16, body)
+
+    def product(slots, start, count):
+        def body(position):
+            rows = pl.ds(start * STRIDE + position, count, stride=STRIDE)
+            left_side = pf[rows, :].astype(BF16)
+            right_side = [rr[slot, position] for slot in slots]
+            right_side = right_side[0] if len(slots) == 1 else jnp.concatenate(right_side, axis=1)
+            result = jnp.dot(left_side, right_side, preferred_element_type=F32)
+            for order, slot in enumerate(slots):
+                (b0, b1)[slot][rows, :] = result[:, order * 128 : (order + 1) * 128]
+
+        loop(LAYER, 32, body)
+
+    owners = (part, left, right, opposite)
+
+    def keep_off(slot, half, coarse_row, rows):
+        start = slot * BS + coarse_row
+        off[half][pl.ds(start, PART, stride=CSTRIDE), :] = rows
+
+    def finish_outer(place):
+        def body(coarse):
+            block = b1[group_rows(place * PART + coarse), :]
+            coarse_row = owners[place] * PART + coarse
+            high = block.astype(BF16)
+            low = (block - high.astype(F32)).astype(BF16)
+            turned = high.T.astype(F32)
+            fixed = turned[:64] + low.T[:64].astype(F32)
+            for half in range(2):
+                base = 16 * half
+                own[half, pl.ds(coarse_row, PART, stride=OSTRIDE), :] = (
+                    fixed[base : base + 16] + fixed[base + 32 : base + 48]
+                )
+                keep_off(4, half, coarse_row, turned[base + 64 : base + 80])
+                keep_off(5, half, coarse_row, turned[base + 96 : base + 112])
+
+        loop(PART, 16, body)
+
+    wide(pc, None, 0)
     for copy in first_half:
         copy.wait_send()
     for copy in second_half:
         copy.wait()
-    wide(gath, 0, left)
-    wide(gath, 1, right)
+    wide(gath, 0, 1)
+    wide(gath, 1, 2)
+    product((0, 1), 0, 3 * PART)
+    for place in range(3):
+        finish_outer(place)
     for copy in relays:
         copy.wait()
-    wide(gath, 2, opposite)
-
-    def product(position):
-        left_side = pf[of_position(position), :].astype(BF16)
-        right_side = jnp.concatenate([rr[0, position], rr[1, position]], axis=1)
-        result = jnp.dot(left_side, right_side, preferred_element_type=F32)
-        b0[of_position(position), :] = result[:, :128]
-        b1[of_position(position), :] = result[:, 128:]
-
-    loop(LAYER, 8, product)
-
-    def keep_off(slot, half, coarse_row, rows):
-        start = slot * BS + coarse_row
-        off[half][pl.ds(start, PART, stride=CSTRIDE), :] = rows
-
-    def finish_outer(coarse_row):
-        block = b1[group_rows(coarse_row), :]
-        high = block.astype(BF16)
-        low = (block - high.astype(F32)).astype(BF16)
-        turned = high.T.astype(F32)
-        fixed = turned[:64] + low.T[:64].astype(F32)
-        for half in range(2):
-            rows = [turned[32 * j + 16 * half : 32 * j + 16 * half + 16] for j in range(4)]
-            own[half, pl.ds(coarse_row, PART, stride=OSTRIDE), :] = (
-                fixed[16 * half : 16 * half + 16] + fixed[32 + 16 * half : 48 + 16 * half]
-            )
-            keep_off(4, half, coarse_row, rows[2])
-            keep_off(5, half, coarse_row, rows[3])
-
-    loop(BS, 4, finish_outer)
+    wide(gath, 2, 3)
+    product((1,), 3 * PART, PART)
+    finish_outer(3)
 
     def own_rows():
         return jnp.concatenate(
@@ -364,14 +379,21 @@
     for copy in third:
         copy.start()
 
-    def finish_local(coarse_row):
-        turned = b0[group_rows(coarse_row), :].astype(BF16).T.astype(F32)
-        for half in range(2):
-            for j in range(4):
-                keep_off(j, half, coarse_row, turned[32 * j + 16 * half : 32 * j + 16 * half + 16])
-
-    loop(BS, 4, finish_local)
-
+    product((0,), 3 * PART, PART)
+
+    def finish_local(place):
+        def body(coarse):
+            turned = b0[group_rows(place * PART + coarse), :].astype(BF16).T.astype(F32)
+            coarse_row = owners[place] * PART + coarse
+            for half in range(2):
+                for j in range(4):
+                    base = 32 * j + 16 * half
+                    keep_off(j, half, coarse_row, turned[base : base + 16])
+
+        loop(PART, 16, body)
+
+    for place in range(4):
+        finish_local(place)
     whole = own_rows()
     high = whole.astype(BF16)
     low = (whole - high.astype(F32)).astype(BF16)

time: 52.6 us -> 46 us (0.87)
  Pallas kernels: 51.1 us -> 44.8 us
    pallas_call x1, Pallas kernels: 48.8 us -> 42.6 us  [on_device(): pl.pallas_call(kernel, out_shape=(pltpu.VMEM((BS, PART, rows), BF16), plt...]
where the time goes in v3:
time: 46 us; the launch traced here: 45.4 us
  Pallas kernels  44.8 us (97%)
  between operations  0.64 us (1%)
    pallas_call x1, Pallas kernels, on_device(): pl.pallas_call(kernel, out_shape=(pltpu.VMEM((BS, PART, rows), BF16), plt...  42.6 us
    pallas_call x1, Pallas kernels, on_device(): pl.pallas_call(finish, out_shape=(jax.ShapeDtypeStruct((BS, PART, rows),...  2.24 us

profile of v3, /device:TPU:4, one launch (start us, length us, event | category | flops | bytes accessed | tf_op | source)
XLA Modules:
  0.0 45.4 jit_solution(10446558571136696504)
XLA Ops:
  0.6 42.6 %shard_map.67 = (bf16[64,16,256]{2,1,0:T(8,128)(2,1)S(1)}, f32[2,1280,128]{2,1,0:T(8,128)S(1)}, f32[8448,128]{1,0:T(8,128)S(1)}, f32[8448,128]{1,0:T(8,128)S(1)}) custom-call(bf16[8,64,64,256]{3,2,1,0:T(8,128)(2,1)} %a_hbm.1, bf16[64,16,256]{2,1,0:T(8,128)(2,1)} %t_ref.1, bf16[64,256]{1,0:T(8,128)(2,1)} %s_ref.1, s32[8,256]{1,0:T(8,128)} %col_ref.1), custom_call_target="tpu_custom_call" | custom-call | tf_op jit(solution)/shard_map/pallas_call | solution.py:442
  43.2 2.2 %shard_map.68 = (bf16[64,16,256]{2,1,0:T(8,128)(2,1)}, f32[1024,256]{1,0:T(8,128)}, bf16[96,64,256]{2,1,0:T(8,128)(2,1)}) custom-call(bf16[64,16,256]{2,1,0:T(8,128)(2,1)S(1)} %get-tuple-element.10.p_ref, f32[2,1280,128]{2,1,0:T(8,128)S(1)} %get-tuple-element.11.d_ref, f32[8448,128]{1,0:T(8,128)S(1)} %get-tuple-element.12.low_ref, ...), custom_call_target="tpu_custom_call" | custom-call | tf_op jit(solution)/shard_map/pallas_call | solution.py:479

commit v4 on v3

--- a/solution.py
+++ b/solution.py
@@ -238,7 +238,7 @@
         send(pxl.at[:, :, pl.ds(0, LAYER)], above, 9, (down, part)),
     ]
     second = exchange(1)
-    for copy in (*second, *first_half, *halo, *second_half):
+    for copy in (*first_half, *second_half, *second, *halo):
         copy.start()
 
     spread(lambda fine: [*halves(pxl, fine)] * 4, yx)
@@ -249,10 +249,6 @@
     loop(LAYER, 8, settle)
     fetch(2, 0).wait()
     relay(stage.at[0], (b4, b5))
-    for copy in first_half:
-        copy.wait_recv()
-    for copy in relays:
-        copy.start()
     fetch(3, 1).wait()
 
     def reach(slot, pairs, blocks, position):
@@ -293,6 +289,10 @@
         return [low, high, *halves(other, fine), below[fine], low, high, above[fine]]
 
     spread(outer_rows, b2)
+    for copy in first_half:
+        copy.wait_recv()
+    for copy in relays:
+        copy.start()
 
     def remote_row(position):
         block = b2[of_position(position), :].astype(BF16)

time: 46 us -> 43.6 us (0.948)
  Pallas kernels: 44.8 us -> 42.8 us
    pallas_call x1, Pallas kernels: 42.6 us -> 40.6 us  [on_device(): pl.pallas_call(kernel, out_shape=(pltpu.VMEM((BS, PART, rows), BF16), plt...]
where the time goes in v4:
time: 43.6 us; the launch traced here: 43.5 us
  Pallas kernels  42.8 us (98%)
  between operations  0.64 us (1%)
    pallas_call x1, Pallas kernels, on_device(): pl.pallas_call(kernel, out_shape=(pltpu.VMEM((BS, PART, rows), BF16), plt...  40.6 us
    pallas_call x1, Pallas kernels, on_device(): pl.pallas_call(finish, out_shape=(jax.ShapeDtypeStruct((BS, PART, rows),...  2.24 us

profile of v4, /device:TPU:4, one launch (start us, length us, event | category | flops | bytes accessed | tf_op | source)
XLA Modules:
  0.0 43.5 jit_solution(4979338355861063364)
XLA Ops:
  0.6 40.6 %shard_map.67 = (bf16[64,16,256]{2,1,0:T(8,128)(2,1)S(1)}, f32[2,1280,128]{2,1,0:T(8,128)S(1)}, f32[8448,128]{1,0:T(8,128)S(1)}, f32[8448,128]{1,0:T(8,128)S(1)}) custom-call(bf16[8,64,64,256]{3,2,1,0:T(8,128)(2,1)} %a_hbm.1, bf16[64,16,256]{2,1,0:T(8,128)(2,1)} %t_ref.1, bf16[64,256]{1,0:T(8,128)(2,1)} %s_ref.1, s32[8,256]{1,0:T(8,128)} %col_ref.1), custom_call_target="tpu_custom_call" | custom-call | tf_op jit(solution)/shard_map/pallas_call | solution.py:442
  41.2 2.2 %shard_map.68 = (bf16[64,16,256]{2,1,0:T(8,128)(2,1)}, f32[1024,256]{1,0:T(8,128)}, bf16[96,64,256]{2,1,0:T(8,128)(2,1)}) custom-call(bf16[64,16,256]{2,1,0:T(8,128)(2,1)S(1)} %get-tuple-element.10.p_ref, f32[2,1280,128]{2,1,0:T(8,128)S(1)} %get-tuple-element.11.d_ref, f32[8448,128]{1,0:T(8,128)S(1)} %get-tuple-element.12.low_ref, ...), custom_call_target="tpu_custom_call" | custom-call | tf_op jit(solution)/shard_map/pallas_call | solution.py:479

commit v5 on v4

--- a/solution.py
+++ b/solution.py
@@ -246,7 +246,7 @@
     def settle(position):
         pn[position] = yx[of_position(position), :].astype(BF16)
 
-    loop(LAYER, 8, settle)
+    loop(LAYER, 16, settle)
     fetch(2, 0).wait()
     relay(stage.at[0], (b4, b5))
     fetch(3, 1).wait()
@@ -273,7 +273,10 @@
     def two_lines(index, carry):
         return local_line(2 * index + 1, local_line(2 * index, carry))
 
-    lax.fori_loop(0, GY // 2, two_lines, 0)
+    def four_lines(index, carry):
+        return two_lines(2 * index + 1, two_lines(2 * index, carry))
+
+    lax.fori_loop(0, GY // 4, four_lines, 0)
 
     for copy in second:
         copy.wait()

time: 43.6 us -> 43.6 us (level)
  no operation moved by 1% of the time
where the time goes in v5:
time: 43.6 us; the launch traced here: 43.5 us
  Pallas kernels  42.8 us (98%)
  between operations  0.64 us (1%)
    pallas_call x1, Pallas kernels, on_device(): pl.pallas_call(kernel, out_shape=(pltpu.VMEM((BS, PART, rows), BF16), plt...  40.6 us
    pallas_call x1, Pallas kernels, on_device(): pl.pallas_call(finish, out_shape=(jax.ShapeDtypeStruct((BS, PART, rows),...  2.24 us

profile of v5, /device:TPU:4, one launch (start us, length us, event | category | flops | bytes accessed | tf_op | source)
XLA Modules:
  0.0 43.5 jit_solution(3033647803573563307)
XLA Ops:
  0.6 40.6 %shard_map.67 = (bf16[64,16,256]{2,1,0:T(8,128)(2,1)S(1)}, f32[2,1280,128]{2,1,0:T(8,128)S(1)}, f32[8448,128]{1,0:T(8,128)S(1)}, f32[8448,128]{1,0:T(8,128)S(1)}) custom-call(bf16[8,64,64,256]{3,2,1,0:T(8,128)(2,1)} %a_hbm.1, bf16[64,16,256]{2,1,0:T(8,128)(2,1)} %t_ref.1, bf16[64,256]{1,0:T(8,128)(2,1)} %s_ref.1, s32[8,256]{1,0:T(8,128)} %col_ref.1), custom_call_target="tpu_custom_call" | custom-call | tf_op jit(solution)/shard_map/pallas_call | solution.py:445
  41.2 2.2 %shard_map.68 = (bf16[64,16,256]{2,1,0:T(8,128)(2,1)}, f32[1024,256]{1,0:T(8,128)}, bf16[96,64,256]{2,1,0:T(8,128)(2,1)}) custom-call(bf16[64,16,256]{2,1,0:T(8,128)(2,1)S(1)} %get-tuple-element.10.p_ref, f32[2,1280,128]{2,1,0:T(8,128)S(1)} %get-tuple-element.11.d_ref, f32[8448,128]{1,0:T(8,128)S(1)} %get-tuple-element.12.low_ref, ...), custom_call_target="tpu_custom_call" | custom-call | tf_op jit(solution)/shard_map/pallas_call | solution.py:482
